TPU v7x, 32 devices: a whole 2x2x4 slice. The times are simulated.
32 devices in a mesh: tm: 2 (over y), space: 16 (over z, x, core).
Axes of the slice: x: 2, y: 2, z: 4, core: 2. Of those that a mesh axis runs over, the one named last changes fastest.
Arguments:
- noisy_state: float32 [8, 2, 256, 256], P('tm', None, 'space'), may hold values from -6 to 6
- fresh_noise: float32 [8, 2, 256, 256], P('tm', None, 'space'), may hold values from -6 to 6
- level_index: int32 [1], replicated, may hold values from 1 to 31
- station_obs: float32 [8, 2, 2048], P('tm', None, 'space'), may hold values from -6 to 6
- obs_variance: float32 [2048], P('space'), may hold values from 0.05 to 0.5
- station_owner: int32 [2048, 1], P('space'), may hold values from 0 to 15; in each aligned block of 128 rows (0 to 127, 128 to 255, ...) at most 32 rows name the same one
- station_cell: int32 [2048], P('space'), may hold values from 0 to 4095
- conv_in: bfloat16 [3, 64, 48], replicated, may hold values from -0.5 to 0.5
- conv_mid: bfloat16 [3, 64, 192], replicated, may hold values from -0.25 to 0.25
- conv_res: bfloat16 [3, 64, 192], replicated, may hold values from -0.25 to 0.25
- conv_out: bfloat16 [3, 16, 192], replicated, may hold values from -0.25 to 0.25
- in_bias: float32 [64], replicated, may hold values from -3 to 3
- noise_embed: float32 [64], replicated, may hold values from -3 to 3
- norm_gain: float32 [64], replicated, may hold values from 0.5 to 2
Outputs:
- next_state: float32 [8, 2, 256, 256], P('tm', None, 'space')
Inputs may be any that keep to these rules, and one draw needn't show every extreme that they name: `station_owner`: among the stations of one device (each aligned block of 128 stations) at most 32 have the same owner strip; every strip owns some station.
All inputs are finite; a program needn't handle non-finite values.
Results may differ from a plain program's by a relative error of at most 0.0023.
Values may be sent and summed in bfloat16 or wider, within the bound.
A program may use at most 64 MiB of HBM per device.

v0:
```python
import jax
import jax.numpy as jnp
from jax import lax
from jax.sharding import PartitionSpec as P

WIN = 8
LEVELS = 32
STRIDE = 4
CHAN = 16


def extended_2(cells, sides, width):
    for axis, dim in sides:
        count = lax.axis_size(axis)
        head = lax.slice_in_dim(cells, 0, width, axis=dim)
        tail = lax.slice_in_dim(cells, cells.shape[dim] - width, cells.shape[dim], axis=dim)
        cells = jnp.concatenate(
            [
                lax.ppermute(tail, axis, [(i, (i + 1) % count) for i in range(count)]),
                cells,
                lax.ppermute(head, axis, [((i + 1) % count, i) for i in range(count)]),
            ],
            axis=dim,
        )
    return cells


def shifted(value, axis, steps):
    count = lax.axis_size(axis)
    first, last = (max(0, -steps), min(count, count - steps))
    return lax.ppermute(value, axis, [(source, source + steps) for source in range(first, last)])


def scale_at(level):
    return 0.3 * jnp.exp(jnp.log(5.0) * level.astype(jnp.float32) / (LEVELS - 1))


def conv_rows(weight, padded):
    out_rows = padded.shape[2] - 2
    stacked = jnp.concatenate(
        [jnp.roll(padded, 1 - col_tap, axis=3) for col_tap in range(3)], axis=1
    )
    total = None
    for row_tap in range(3):
        product = jnp.einsum(
            "oc,ncyx->noyx",
            weight[row_tap],
            stacked[:, :, row_tap : row_tap + out_rows, :],
            preferred_element_type=jnp.float32,
        )
        total = product if total is None else total + product
    return total


def hidden_rim(hidden):
    return extended_2(hidden, (("space", 2),), 1)


def score_net(windows, conv_in, conv_mid, conv_res, conv_out, bias, norm_gain):
    source = extended_2(windows, (("space", 2),), 1)
    first = jax.nn.silu(conv_rows(conv_in, source) + bias[None, :, None, None]).astype(jnp.bfloat16)
    middle = conv_rows(conv_mid, hidden_rim(first))
    normed = (
        middle
        * lax.rsqrt(jnp.mean(middle * middle, axis=1, keepdims=True) + 1e-05)
        * norm_gain[None, :, None, None]
    )
    second = jax.nn.silu(normed).astype(jnp.bfloat16)
    branch = jax.nn.silu(conv_rows(conv_res, hidden_rim(second)))
    third = (first.astype(jnp.float32) + branch).astype(jnp.bfloat16)
    return conv_rows(conv_out, hidden_rim(third))


def local(
    noisy_state,
    fresh_noise,
    level_index,
    station_obs,
    obs_variance,
    station_owner,
    station_cell,
    conv_in,
    conv_mid,
    conv_res,
    conv_out,
    in_bias,
    noise_embed,
    norm_gain,
):
    step_count, layer_count, row_count, col_count = noisy_state.shape
    noise_scale = scale_at(level_index[0])
    next_scale = scale_at(level_index[0] - 1)
    bias = in_bias + noise_embed * jnp.log(10.0 * noise_scale)
    scaled = (noisy_state / jnp.sqrt(1.0 + noise_scale * noise_scale)).astype(jnp.bfloat16)
    time_rank = lax.axis_index("tm")
    total_steps = step_count * lax.axis_size("tm")
    ahead = shifted(scaled, "tm", -1)
    extended = jnp.concatenate([scaled, ahead], axis=0)
    offset = 0
    window_count = (extended.shape[0] - WIN) // STRIDE + 1
    windows = jnp.stack([extended])
    windows = windows.reshape(window_count, CHAN, row_count, col_count)
    outputs = score_net(windows, conv_in, conv_mid, conv_res, conv_out, bias, norm_gain)
    starts = time_rank * step_count - offset + STRIDE * jnp.arange(window_count, dtype=jnp.int32)
    usable = ((starts >= 0) & (starts + WIN <= total_steps)).astype(jnp.float32)
    halves = (
        outputs.reshape(window_count, 2, STRIDE, layer_count, row_count, col_count)
        * usable[:, None, None, None, None, None]
    )
    blank = jnp.zeros((1, STRIDE, layer_count, row_count, col_count), jnp.float32)
    summed = jnp.concatenate([halves[:, 0], blank], axis=0) + jnp.concatenate(
        [blank, halves[:, 1]], axis=0
    )
    summed = summed.reshape(extended.shape[0], layer_count, row_count, col_count)
    spill = shifted(summed[step_count:], "tm", 1)
    own = jnp.concatenate([summed[:STRIDE] + spill, summed[STRIDE:step_count]], axis=0)
    moment = time_rank * step_count + jnp.arange(step_count, dtype=jnp.int32)
    cover = jnp.where((moment < STRIDE) | (moment >= total_steps - STRIDE), 1.0, 2.0).astype(
        jnp.float32
    )
    estimate = noisy_state - noise_scale * (own / cover[:, None, None, None])
    space_size = lax.axis_size("space")
    station_count = station_cell.shape[0]
    capacity = 4 * station_count // space_size
    values = station_obs.reshape(step_count * layer_count, station_count)
    target = station_owner[:, 0]
    earlier = lax.broadcasted_iota(
        jnp.int32, (station_count, station_count), 0
    ) < lax.broadcasted_iota(jnp.int32, (station_count, station_count), 1)
    ranked = jnp.sum(
        jnp.where((target[:, None] == target[None, :]) & earlier, 1, 0), axis=0
    ).astype(jnp.int32)
    slot = target * capacity + ranked
    slot_count = space_size * capacity
    value_slots = jnp.zeros((values.shape[0], slot_count), jnp.float32).at[:, slot].set(values)
    spread_slots = jnp.zeros((1, slot_count), jnp.float32).at[0, slot].set(obs_variance)
    cell_slots = jnp.full((1, slot_count), -1, jnp.int32).at[0, slot].set(station_cell)
    got_values, got_spread, got_cells = (
        lax.all_to_all(value_slots, "space", split_axis=1, concat_axis=1, tiled=True),
        lax.all_to_all(spread_slots, "space", split_axis=1, concat_axis=1, tiled=True),
        lax.all_to_all(cell_slots, "space", split_axis=1, concat_axis=1, tiled=True),
    )
    present = got_cells[0] >= 0
    spot = jnp.maximum(got_cells[0], 0)
    flat = estimate.reshape(step_count * layer_count, row_count * col_count)
    seen = jnp.take(flat, spot, axis=1)
    misfit = jnp.where(
        present[None, :], (got_values - seen) / (got_spread + noise_scale * noise_scale), 0.0
    )
    pull = jnp.zeros_like(flat).at[:, spot].add(misfit)
    return (
        estimate
        + noise_scale * noise_scale * pull.reshape(estimate.shape)
        + next_scale * fresh_noise
    )


def solution(mesh):
    placed = (
        P("tm", None, "space", None),
        P("tm", None, "space", None),
        P(),
        P("tm", None, "space"),
        P("space"),
        P("space", None),
        P("space"),
        P(),
        P(),
        P(),
        P(),
        P(),
        P(),
        P(),
    )
    return jax.shard_map(
        local, mesh=mesh, in_specs=placed, out_specs=P("tm", None, "space", None), check_vma=False
    )
```

profile of v0, /device:TPU:0, one launch (start us, length us, event | category | flops | bytes accessed | tf_op | source)
XLA Modules:
  0.0 82.8 jit_solution(5439972341782676317)
XLA Ops:
  0.8 0.9 %divide_convert_fusion = bf16[4,2,16,256]{3,2,1,0:T(8,128)(2,1)S(1)} fusion(f32[4,2,16,256]{3,2,1,0:T(8,128)} %param.14, f32[]{:T(128)S(6)} %sqrt.3), kind=kLoop, calls=%fused_computation.84 | loop fusion | flops 65536 | bytes 196612 | tf_op jit(solution)/shard_map/convert_element_type | solution.py:94
  1.7 1.3 %collective-permute-start = (bf16[4,2,16,256]{3,2,1,0:T(8,128)(2,1)S(1)}, bf16[4,2,16,256]{3,2,1,0:T(8,128)(2,1)S(1)}, u32[]{:S(2)}, u32[]{:S(2)}) collective-permute-start(bf16[4,2,16,256]{3,2,1,0:T(8,128)(2,1)S(1)} %divide_convert_fusion), channel_id=1, source_target_pairs={{16,0},{17,1},{18,2},{19,3},{20,4},{21,5},{22,6},{23,7},{24,8},{25... | collective-permute-start | bytes 196616 | tf_op jit(solution)/shard_map/ppermute | solution.py:31
  3.0 0.8 select_reduce_fusion
  3.8 0.7 fusion.78
  4.5 1.1 %scatter_custom_fusion = s32[512]{0:T(512)S(1)} fusion(s32[128]{0:T(128)S(1)} %fusion.78, s32[128]{0:T(128)} %param.20, s32[]{:T(128)} %constant.78.clone.1), kind=kCustom, calls=%fused_computation.129 | custom fusion | bytes 2560 | tf_op jit(solution)/shard_map/scatter | solution.py:137
  5.6 0.7 all_to_all.20
  6.3 7.4 %all-to-all-start = ((s32[1,16,32]{2,0,1:T(1,128)}), s32[1,16,32]{2,0,1:T(1,128)S(1)}, u32[]{:S(2)}, u32[]{:S(2)}) async-start(s32[1,16,32]{2,0,1:T(1,128)} %all_to_all.20), calls=%async_computation | async-start | bytes 16384 | tf_op jit(solution)/shard_map/all_to_all | solution.py:141
  14.3 0.7 multiply_add_fusion.1
  14.9 4.1 %collective-permute-start.2 = (bf16[1,16,1,256]{3,1,2,0:T(8,128)(2,1)S(1)}, bf16[1,16,1,256]{3,1,2,0:T(8,128)(2,1)S(1)}, u32[]{:S(2)}, u32[]{:S(2)}) collective-permute-start(bf16[1,16,1,256]{3,1,2,0:T(8,128)(2,1)S(1)} %copy.65), channel_id=1, source_target_pairs={{1,0},{2,1},{3,2},{4,3},{5,4},{6,5},{7,6},{8,7},{9,8},{10,9},{11,1... | collective-permute-start | bytes 24584 | tf_op jit(solution)/shard_map/ppermute | solution.py:21
  19.0 0.6 collective-permute-done.1
  19.7 0.7 collective-permute-done.2
  22.0 4.5 %collective-permute-start.4 = (bf16[1,64,1,256]{3,1,2,0:T(8,128)(2,1)S(1)}, bf16[1,64,1,256]{3,1,2,0:T(8,128)(2,1)S(1)}, u32[]{:S(2)}, u32[]{:S(2)}) collective-permute-start(bf16[1,64,1,256]{3,1,2,0:T(8,128)(2,1)S(1)} %get-tuple-element.24), channel_id=1, source_target_pairs={{1,0},{2,1},{3,2},{4,3},{5,4},{6,5},{7,6},{8,7},{9,8},{10,9},{11,1... | collective-permute-start | bytes 98312 | tf_op jit(solution)/shard_map/ppermute | solution.py:21
  26.5 1.1 %scatter_custom_fusion.2 = f32[512]{0:T(512)S(1)} fusion(s32[128]{0:T(128)S(1)} %fusion.78, f32[128]{0:T(128)} %param.18, f32[]{:T(128)} %constant.35.clone.1), kind=kCustom, calls=%fused_computation.127 | custom fusion | bytes 2560 | tf_op jit(solution)/shard_map/scatter | solution.py:136
  27.6 0.7 all_to_all.25
  28.4 0.9 %scatter_custom_fusion.1 = f32[8,512]{0,1:T(8,128)S(1)} fusion(s32[128]{0:T(128)S(1)} %fusion.78, f32[]{:T(128)} %constant.35.clone.1, f32[8,128]{0,1:T(8,128)S(1)} %copy.54), kind=kCustom, calls=%fused_computation.82 | custom fusion | bytes 81924 | tf_op jit(solution)/shard_map/scatter | solution.py:135
  29.5 0.7 reshape.297
  30.8 1.4 %maximum_maximum_fusion = bf16[1,192,18,256]{3,1,2,0:T(8,128)(2,1)S(1)} fusion(bf16[1,64,18,1]{3,1,2,0:T(8,128)(2,1)S(1)} %get-tuple-element.16, bf16[1,64,18,255]{3,1,2,0:T(8,128)(2,1)S(1)} %get-tuple-element.18, bf16[1,64,1,256]{3,1,2,0:T(8,128)(2,1)S(1)} %collective-permute-done.4, bf16[1,64,16,256]{3,1,2,0:T(8,128)(2,1)S(1)} %multiply_convert_fusion, ...), kind=kLoop, calls=%fused_computation.5 | loop fusion | flops 12386304 | bytes 3538944 | tf_op jit(solution)/shard_map/concatenate | solution.py:40
  34.2 4.4 %collective-permute-start.6 = (bf16[1,64,1,256]{3,1,2,0:T(8,128)(2,1)S(1)}, bf16[1,64,1,256]{3,1,2,0:T(8,128)(2,1)S(1)}, u32[]{:S(2)}, u32[]{:S(2)}) collective-permute-start(bf16[1,64,1,256]{3,1,2,0:T(8,128)(2,1)S(1)} %get-tuple-element.22), channel_id=1, source_target_pairs={{1,0},{2,1},{3,2},{4,3},{5,4},{6,5},{7,6},{8,7},{9,8},{10,9},{11,1... | collective-permute-start | bytes 98312 | tf_op jit(solution)/shard_map/ppermute | solution.py:21
  38.6 3.4 %all-to-all-start.2 = ((f32[1,16,32]{2,0,1:T(1,128)}), f32[1,16,32]{2,0,1:T(1,128)S(1)}, u32[]{:S(2)}, u32[]{:S(2)}) async-start(f32[1,16,32]{2,0,1:T(1,128)} %all_to_all.25), calls=%async_computation.2 | async-start | bytes 16384 | tf_op jit(solution)/shard_map/all_to_all | solution.py:140
  42.7 1.4 %maximum_maximum_fusion.1 = bf16[1,192,18,256]{3,1,2,0:T(8,128)(2,1)S(1)} fusion(bf16[1,64,18,1]{3,1,2,0:T(8,128)(2,1)S(1)} %get-tuple-element.12, bf16[1,64,18,255]{3,1,2,0:T(8,128)(2,1)S(1)} %get-tuple-element.14, bf16[1,64,1,256]{3,1,2,0:T(8,128)(2,1)S(1)} %collective-permute-done.6, bf16[1,64,16,256]{3,1,2,0:T(8,128)(2,1)S(1)} %fusion.27, ...), kind=kLoop, calls=%fused_computation.6 | loop fusion | flops 12386304 | bytes 3538944 | tf_op jit(solution)/shard_map/concatenate | solution.py:40
  44.9 0.6 add_convert_fusion
  45.9 4.2 %collective-permute-start.8 = (bf16[1,64,1,256]{3,1,2,0:T(8,128)(2,1)S(1)}, bf16[1,64,1,256]{3,1,2,0:T(8,128)(2,1)S(1)}, u32[]{:S(2)}, u32[]{:S(2)}) collective-permute-start(bf16[1,64,1,256]{3,1,2,0:T(8,128)(2,1)S(1)} %get-tuple-element.20), channel_id=1, source_target_pairs={{1,0},{2,1},{3,2},{4,3},{5,4},{6,5},{7,6},{8,7},{9,8},{10,9},{11,1... | collective-permute-start | bytes 98312 | tf_op jit(solution)/shard_map/ppermute | solution.py:21
  50.1 1.6 %collective-permute-done.7 = bf16[1,64,1,256]{3,1,2,0:T(8,128)(2,1)S(1)} collective-permute-done((bf16[1,64,1,256]{3,1,2,0:T(8,128)(2,1)S(1)}, bf16[1,64,1,256]{3,1,2,0:T(8,128)(2,1)S(1)}, u32[]{:S(2)}, u32[]{:S(2)}) %collective-permute-start.7) | collective-permute-done | bytes 32800 | tf_op jit(solution)/shard_map/ppermute | solution.py:19
  52.2 1.4 %maximum_maximum_fusion.2 = bf16[1,192,18,256]{3,1,2,0:T(8,128)(2,1)S(1)} fusion(bf16[1,64,18,1]{3,1,2,0:T(8,128)(2,1)S(1)} %get-tuple-element.8, bf16[1,64,18,255]{3,1,2,0:T(8,128)(2,1)S(1)} %get-tuple-element.10, bf16[1,64,1,256]{3,1,2,0:T(8,128)(2,1)S(1)} %collective-permute-done.8, bf16[1,64,16,256]{3,1,2,0:T(8,128)(2,1)S(1)} %add_convert_fusion, ...), kind=kLoop, calls=%fused_computation.7 | loop fusion | flops 12386304 | bytes 3538944 | tf_op jit(solution)/shard_map/concatenate | solution.py:40
  54.8 4.5 %collective-permute-start.9 = (f32[4,2,16,256]{3,2,1,0:T(8,128)S(1)}, f32[4,2,16,256]{3,2,1,0:T(8,128)S(1)}, u32[]{:S(2)}, u32[]{:S(2)}) collective-permute-start(f32[4,2,16,256]{3,2,1,0:T(8,128)S(1)} %fusion.40), channel_id=1, source_target_pairs={{0,16},{1,17},{2,18},{3,19},{4,20},{5,21},{6,22},{7,23},{8,24},{9,... | collective-permute-start | bytes 393224 | tf_op jit(solution)/shard_map/ppermute | solution.py:31
  59.3 5.6 %all-to-all-start.1 = ((f32[16,1,256]{2,1,0:T(1,128)}), f32[16,1,256]{2,1,0:T(1,128)S(1)}, u32[]{:S(2)}, u32[]{:S(2)}) async-start(f32[16,1,256]{2,1,0:T(1,128)} %reshape.297), calls=%async_computation.1 | async-start | bytes 32768 | tf_op jit(solution)/shard_map/all_to_all | solution.py:139
  65.3 6.1 %all-to-all-done.1 = f32[16,1,256]{2,1,0:T(1,128)S(1)} async-done(((f32[16,1,256]{2,1,0:T(1,128)}), f32[16,1,256]{2,1,0:T(1,128)S(1)}, u32[]{:S(2)}, u32[]{:S(2)}) %all-to-all-start.1) | async-done | bytes 16416 | tf_op jit(solution)/shard_map/all_to_all | solution.py:139
  71.9 0.7 reduce.14
  73.0 0.6 copy.57
  73.6 6.2 %scatter_custom_fusion.3 = f32[8,4096]{0,1:T(8,128)} fusion(s32[512]{0:T(512)S(1)} %reshape.243, f32[]{:T(128)} %constant.35.clone.1, f32[8,512]{0,1:T(8,128)S(1)} %bitcast.203, f32[]{:T(128)} %constant.83.clone.1, f32[512]{0:T(512)S(1)} %add.188, pred[512]{0:T(512)(128)(4,1)S(1)} %le.21, pred[512]{0:T(512)(128)(4,1)S(1)} %ge.31, f32[8,4096]{0,1:T(8,128)S(1)} %copy.57, ...), kind=kCustom, calls=%fused_computation.46 | custom fusion | flops 20480 | bytes 2499072 | tf_op jit(solution)/shard_map/scatter-add | solution.py:150
  79.8 2.2 %copy.58 = f32[8,4096]{1,0:T(8,128)S(1)} copy(f32[8,4096]{0,1:T(8,128)} %scatter_custom_fusion.3) | data formatting | bytes 262144 | tf_op jit(solution)/shard_map/scatter-add | solution.py:150
  82.1 0.7 multiply_add_fusion
  (85 shorter events, 9.7 us)
Async XLA Ops:
  0.0 20.7 %copy-start.5 = (bf16[3,64,48]{1,2,0:T(8,128)(2,1)S(1)}, bf16[3,64,48]{1,2,0:T(8,128)(2,1)}, u32[]{:S(2)}) copy-start(bf16[3,64,48]{1,2,0:T(8,128)(2,1)} %param.21) | copy-start | bytes 55300
  1.7 12.0 %collective-permute-start = (bf16[4,2,16,256]{3,2,1,0:T(8,128)(2,1)S(1)}, bf16[4,2,16,256]{3,2,1,0:T(8,128)(2,1)S(1)}, u32[]{:S(2)}, u32[]{:S(2)}) collective-permute-start(bf16[4,2,16,256]{3,2,1,0:T(8,128)(2,1)S(1)} %divide_convert_fusion), channel_id=1, source_target_pairs={{16,0},{17,1},{18,2},{19,3},{20,4},{21,5},{22,6},{23,7},{24,8},{25... | collective-permute-start | bytes 196616 | tf_op jit(solution)/shard_map/ppermute | solution.py:31
  6.3 32.3 %all-to-all-start = ((s32[1,16,32]{2,0,1:T(1,128)}), s32[1,16,32]{2,0,1:T(1,128)S(1)}, u32[]{:S(2)}, u32[]{:S(2)}) async-start(s32[1,16,32]{2,0,1:T(1,128)} %all_to_all.20), calls=%async_computation | async-start | bytes 16384 | tf_op jit(solution)/shard_map/all_to_all | solution.py:141
  13.8 5.8 %collective-permute-start.1 = (bf16[1,16,1,256]{3,1,2,0:T(8,128)(2,1)S(1)}, bf16[1,16,1,256]{3,1,2,0:T(8,128)(2,1)S(1)}, u32[]{:S(2)}, u32[]{:S(2)}) collective-permute-start(bf16[1,16,1,256]{3,1,2,0:T(8,128)(2,1)S(1)} %copy.64), channel_id=1, source_target_pairs={{0,1},{1,2},{2,3},{3,4},{4,5},{5,6},{6,7},{7,8},{8,9},{9,10},{10,1... | collective-permute-start | bytes 24584 | tf_op jit(solution)/shard_map/ppermute | solution.py:19
  14.9 5.4 %collective-permute-start.2 = (bf16[1,16,1,256]{3,1,2,0:T(8,128)(2,1)S(1)}, bf16[1,16,1,256]{3,1,2,0:T(8,128)(2,1)S(1)}, u32[]{:S(2)}, u32[]{:S(2)}) collective-permute-start(bf16[1,16,1,256]{3,1,2,0:T(8,128)(2,1)S(1)} %copy.65), channel_id=1, source_target_pairs={{1,0},{2,1},{3,2},{4,3},{5,4},{6,5},{7,6},{8,7},{9,8},{10,9},{11,1... | collective-permute-start | bytes 24584 | tf_op jit(solution)/shard_map/ppermute | solution.py:21
  21.4 6.9 %copy-start.6 = (f32[4,2,128]{2,1,0:T(2,128)S(1)}, f32[4,2,128]{2,1,0:T(2,128)}, u32[]{:S(2)}) copy-start(f32[4,2,128]{2,1,0:T(2,128)} %param.17) | copy-start | bytes 12292
  22.0 8.3 %collective-permute-start.3 = (bf16[1,64,1,256]{3,1,2,0:T(8,128)(2,1)S(1)}, bf16[1,64,1,256]{3,1,2,0:T(8,128)(2,1)S(1)}, u32[]{:S(2)}, u32[]{:S(2)}) collective-permute-start(bf16[1,64,1,256]{3,1,2,0:T(8,128)(2,1)S(1)} %get-tuple-element.23), channel_id=1, source_target_pairs={{0,1},{1,2},{2,3},{3,4},{4,5},{5,6},{6,7},{7,8},{8,9},{9,10},{10,1... | collective-permute-start | bytes 98312 | tf_op jit(solution)/shard_map/ppermute | solution.py:19
  22.0 8.2 %collective-permute-start.4 = (bf16[1,64,1,256]{3,1,2,0:T(8,128)(2,1)S(1)}, bf16[1,64,1,256]{3,1,2,0:T(8,128)(2,1)S(1)}, u32[]{:S(2)}, u32[]{:S(2)}) collective-permute-start(bf16[1,64,1,256]{3,1,2,0:T(8,128)(2,1)S(1)} %get-tuple-element.24), channel_id=1, source_target_pairs={{1,0},{2,1},{3,2},{4,3},{5,4},{6,5},{7,6},{8,7},{9,8},{10,9},{11,1... | collective-permute-start | bytes 98312 | tf_op jit(solution)/shard_map/ppermute | solution.py:21
  30.8 1.4 %copy-start.2 = (bf16[3,64,192]{2,1,0:T(8,128)(2,1)S(1)}, bf16[3,64,192]{2,1,0:T(8,128)(2,1)}, u32[]{:S(2)}) copy-start(bf16[3,64,192]{2,1,0:T(8,128)(2,1)} %param.22) | copy-start | bytes 221188
  33.0 0.7 copy-start.7
  34.1 8.0 %collective-permute-start.5 = (bf16[1,64,1,256]{3,1,2,0:T(8,128)(2,1)S(1)}, bf16[1,64,1,256]{3,1,2,0:T(8,128)(2,1)S(1)}, u32[]{:S(2)}, u32[]{:S(2)}) collective-permute-start(bf16[1,64,1,256]{3,1,2,0:T(8,128)(2,1)S(1)} %get-tuple-element.21), channel_id=1, source_target_pairs={{0,1},{1,2},{2,3},{3,4},{4,5},{5,6},{6,7},{7,8},{8,9},{9,10},{10,1... | collective-permute-start | bytes 98312 | tf_op jit(solution)/shard_map/ppermute | solution.py:19
  34.2 8.0 %collective-permute-start.6 = (bf16[1,64,1,256]{3,1,2,0:T(8,128)(2,1)S(1)}, bf16[1,64,1,256]{3,1,2,0:T(8,128)(2,1)S(1)}, u32[]{:S(2)}, u32[]{:S(2)}) collective-permute-start(bf16[1,64,1,256]{3,1,2,0:T(8,128)(2,1)S(1)} %get-tuple-element.22), channel_id=1, source_target_pairs={{1,0},{2,1},{3,2},{4,3},{5,4},{6,5},{7,6},{8,7},{9,8},{10,9},{11,1... | collective-permute-start | bytes 98312 | tf_op jit(solution)/shard_map/ppermute | solution.py:21
  38.6 20.7 %all-to-all-start.2 = ((f32[1,16,32]{2,0,1:T(1,128)}), f32[1,16,32]{2,0,1:T(1,128)S(1)}, u32[]{:S(2)}, u32[]{:S(2)}) async-start(f32[1,16,32]{2,0,1:T(1,128)} %all_to_all.25), calls=%async_computation.2 | async-start | bytes 16384 | tf_op jit(solution)/shard_map/all_to_all | solution.py:140
  42.7 1.4 %copy-start.3 = (bf16[3,64,192]{2,1,0:T(8,128)(2,1)S(1)}, bf16[3,64,192]{2,1,0:T(8,128)(2,1)}, u32[]{:S(2)}) copy-start(bf16[3,64,192]{2,1,0:T(8,128)(2,1)} %param.23) | copy-start | bytes 221188
  45.5 6.1 %collective-permute-start.7 = (bf16[1,64,1,256]{3,1,2,0:T(8,128)(2,1)S(1)}, bf16[1,64,1,256]{3,1,2,0:T(8,128)(2,1)S(1)}, u32[]{:S(2)}, u32[]{:S(2)}) collective-permute-start(bf16[1,64,1,256]{3,1,2,0:T(8,128)(2,1)S(1)} %get-tuple-element.19), channel_id=1, source_target_pairs={{0,1},{1,2},{2,3},{3,4},{4,5},{5,6},{6,7},{7,8},{8,9},{9,10},{10,1... | collective-permute-start | bytes 98312 | tf_op jit(solution)/shard_map/ppermute | solution.py:19
  45.9 5.8 %collective-permute-start.8 = (bf16[1,64,1,256]{3,1,2,0:T(8,128)(2,1)S(1)}, bf16[1,64,1,256]{3,1,2,0:T(8,128)(2,1)S(1)}, u32[]{:S(2)}, u32[]{:S(2)}) collective-permute-start(bf16[1,64,1,256]{3,1,2,0:T(8,128)(2,1)S(1)} %get-tuple-element.20), channel_id=1, source_target_pairs={{1,0},{2,1},{3,2},{4,3},{5,4},{6,5},{7,6},{8,7},{9,8},{10,9},{11,1... | collective-permute-start | bytes 98312 | tf_op jit(solution)/shard_map/ppermute | solution.py:21
  52.2 1.4 %copy-start.4 = (bf16[3,16,192]{2,1,0:T(8,128)(2,1)S(1)}, bf16[3,16,192]{2,1,0:T(8,128)(2,1)}, u32[]{:S(2)}) copy-start(bf16[3,16,192]{2,1,0:T(8,128)(2,1)} %param.24) | copy-start | bytes 55300
  54.2 18.6 %copy-start = (f32[4,2,16,256]{3,2,1,0:T(8,128)S(1)}, f32[4,2,16,256]{3,2,1,0:T(8,128)}, u32[]{:S(2)}) copy-start(f32[4,2,16,256]{3,2,1,0:T(8,128)} %param.14) | copy-start | bytes 393220
  54.8 18.0 %collective-permute-start.9 = (f32[4,2,16,256]{3,2,1,0:T(8,128)S(1)}, f32[4,2,16,256]{3,2,1,0:T(8,128)S(1)}, u32[]{:S(2)}, u32[]{:S(2)}) collective-permute-start(f32[4,2,16,256]{3,2,1,0:T(8,128)S(1)} %fusion.40), channel_id=1, source_target_pairs={{0,16},{1,17},{2,18},{3,19},{4,20},{5,21},{6,22},{7,23},{8,24},{9,... | collective-permute-start | bytes 393224 | tf_op jit(solution)/shard_map/ppermute | solution.py:31
  59.3 12.1 %all-to-all-start.1 = ((f32[16,1,256]{2,1,0:T(1,128)}), f32[16,1,256]{2,1,0:T(1,128)S(1)}, u32[]{:S(2)}, u32[]{:S(2)}) async-start(f32[16,1,256]{2,1,0:T(1,128)} %reshape.297), calls=%async_computation.1 | async-start | bytes 32768 | tf_op jit(solution)/shard_map/all_to_all | solution.py:139
  79.8 2.3 %copy-start.1 = (f32[4,2,16,256]{3,2,1,0:T(8,128)S(1)}, f32[4,2,16,256]{3,2,1,0:T(8,128)}, u32[]{:S(2)}) copy-start(f32[4,2,16,256]{3,2,1,0:T(8,128)} %param.15) | copy-start | bytes 393220
where the time goes:
time: 83.3 us; the launch traced here: 82.8 us
  starting transfers between devices  40.3 us (48%)
  other arithmetic  15.8 us (19%)
  local copies, waits for them, and re-layouts  11.5 us (14%)
  waiting for transfers between devices  9.03 us (11%)
  matrix products  4.83 us (6%)
  between operations  1.38 us (2%)
    ppermute x4, starting transfers between devices, extended_2(): lax.ppermute(head, axis, [((i + 1) % count, i) for i in range(count)])  17.1 us
    all_to_all x1, starting transfers between devices, local(): lax.all_to_all(cell_slots, 'space', split_axis=1, concat_axis=1, tiled=True)  7.39 us
    scatter-add x1, other arithmetic, local(): pull = jnp.zeros_like(flat).at[:, spot].add(misfit)  6.21 us
    all_to_all x1, waiting for transfers between devices, local(): lax.all_to_all(value_slots, 'space', split_axis=1, concat_axis=1, tiled=T...  6.12 us
    ppermute x2, starting transfers between devices, shifted(): lax.ppermute(value, axis, [(source, source + steps) for source in range(f...  5.84 us
    all_to_all x1, starting transfers between devices, local(): lax.all_to_all(value_slots, 'space', split_axis=1, concat_axis=1, tiled=T...  5.56 us
    dot_general x12, matrix products, conv_rows(): jnp.einsum('oc,ncyx->noyx', weight[row_tap], stacked[:, :, row_tap:row_ta...  4.83 us
    concatenate x4, other arithmetic, conv_rows(): jnp.concatenate([jnp.roll(padded, 1 - col_tap, axis=3) for col_tap in ran...  4.2 us
  transfers between devices with their start and end apart: 13, of which 4 were waited for; matrix products, arithmetic and copies ran while one was open for 24% of the time, Pallas kernels for 0%

commit v1 on v0

--- a/solution.py
+++ b/solution.py
@@ -1,6 +1,8 @@
 import jax
 import jax.numpy as jnp
 from jax import lax
+from jax.experimental import pallas as pl
+from jax.experimental.pallas import tpu as pltpu
 from jax.sharding import PartitionSpec as P
 
 WIN = 8
@@ -155,6 +157,305 @@
     )
 
 
+MESH = pl.DeviceIdType.MESH
+HALO = 4
+
+
+def gate(v):
+    return 0.5 * v * (jnp.tanh(0.5 * v) + 1.0)
+
+
+def with_neighbours(v):
+    cols = v.shape[1]
+    return jnp.concatenate(
+        [pltpu.roll(v, 1, axis=1), v, pltpu.roll(v, cols - 1, axis=1)], axis=0
+    ).astype(jnp.bfloat16)
+
+
+def fused_kernel(
+    space,
+    scaled_ref,
+    pack_ref,
+    w_in_ref,
+    w_mid_ref,
+    w_res_ref,
+    w_out_ref,
+    bias_ref,
+    gain_ref,
+    den_ref,
+    pull_ref,
+    win,
+    sta,
+    cols_in,
+    cols_hid,
+    cols_sec,
+    cols_third,
+    prod,
+    first,
+    result,
+    arrived,
+    left_hand,
+    right_hand,
+    send_halo,
+    recv_halo,
+    send_sta,
+    recv_sta,
+    send_out,
+    recv_out,
+):
+    t = lax.axis_index("tm")
+    s = lax.axis_index("space")
+    peer = 1 - t
+    after = lax.rem(s + 1, space)
+    before = lax.rem(s + space - 1, space)
+    diagonal = lax.rem(s + space - 1 + 2 * t, space)
+    strip = scaled_ref.shape[0]
+    half = strip // 2
+    span = half + HALO
+    chans = scaled_ref.shape[1]
+    hidden = bias_ref.shape[0]
+    width = scaled_ref.shape[2]
+
+    barrier = pltpu.get_barrier_semaphore()
+    pl.semaphore_signal(barrier, inc=1, device_id=(peer, s), device_id_type=MESH)
+    pl.semaphore_signal(barrier, inc=1, device_id=(peer, diagonal), device_id_type=MESH)
+    for d in range(1, space):
+        pl.semaphore_signal(
+            barrier, inc=1, device_id=(t, lax.rem(s + d, space)), device_id_type=MESH
+        )
+    pl.semaphore_wait(barrier, space + 1)
+
+    to_peer = pltpu.make_async_remote_copy(
+        src_ref=scaled_ref.at[pl.ds(HALO * peer, span)],
+        dst_ref=win.at[t, pl.ds(HALO * t, span)],
+        send_sem=send_halo.at[0],
+        recv_sem=recv_halo.at[0],
+        device_id=(peer, s),
+        device_id_type=MESH,
+    )
+    to_after = pltpu.make_async_remote_copy(
+        src_ref=scaled_ref.at[pl.ds(strip - HALO, HALO)],
+        dst_ref=win.at[t, pl.ds(0, HALO)],
+        send_sem=send_halo.at[1],
+        recv_sem=recv_halo.at[1 + t],
+        device_id=(0, after),
+        device_id_type=MESH,
+    )
+    to_before = pltpu.make_async_remote_copy(
+        src_ref=scaled_ref.at[pl.ds(0, HALO)],
+        dst_ref=win.at[t, pl.ds(span, HALO)],
+        send_sem=send_halo.at[2],
+        recv_sem=recv_halo.at[1 + t],
+        device_id=(1, before),
+        device_id_type=MESH,
+    )
+    to_peer.start()
+    to_after.start()
+    to_before.start()
+    station_copies = []
+    for d in range(1, space):
+        copy = pltpu.make_async_remote_copy(
+            src_ref=pack_ref,
+            dst_ref=sta.at[d],
+            send_sem=send_sta.at[d],
+            recv_sem=recv_sta.at[d],
+            device_id=(t, lax.rem(s + d, space)),
+            device_id_type=MESH,
+        )
+        copy.start()
+        station_copies.append(copy)
+    sta[0] = pack_ref[...]
+    win[t, pl.ds(HALO * (1 - t), span)] = scaled_ref[pl.ds(HALO * t, span)]
+
+    def landed(dst, sem):
+        pltpu.make_async_copy(dst, dst, sem).wait()
+
+    landed(win.at[peer, pl.ds(HALO * peer, span)], recv_halo.at[0])
+    edge = span * t
+    landed(win.at[0, pl.ds(edge, HALO)], recv_halo.at[1])
+    landed(win.at[1, pl.ds(edge, HALO)], recv_halo.at[2])
+
+    rows = half + 2 * HALO
+    bias = jnp.broadcast_to(bias_ref[...], (hidden, width))
+    gain = jnp.broadcast_to(gain_ref[...], (hidden, width))
+
+    def products(weight_ref, columns, count):
+        outs = weight_ref.shape[0]
+        for r in range(count):
+            prod[r, :outs] = jnp.dot(
+                weight_ref[...], columns[r], preferred_element_type=jnp.float32
+            )
+
+    def summed(y, outs):
+        return (
+            prod[y, 0:outs] + prod[y + 1, outs : 2 * outs] + prod[y + 2, 2 * outs : 3 * outs]
+        )
+
+    for r in range(rows):
+        both = jnp.concatenate(
+            [win[0, r].astype(jnp.float32), win[1, r].astype(jnp.float32)], axis=0
+        )
+        cols_in[r] = with_neighbours(both)
+    products(w_in_ref, cols_in, rows)
+    for y in range(rows - 2):
+        value = gate(summed(y, hidden) + bias)
+        first[y] = value.astype(jnp.bfloat16)
+        cols_hid[y] = with_neighbours(value)
+    products(w_mid_ref, cols_hid, rows - 2)
+    for y in range(rows - 4):
+        middle = summed(y, hidden)
+        power = jnp.mean(middle * middle, axis=0, keepdims=True)
+        cols_sec[y] = with_neighbours(gate(middle * lax.rsqrt(power + 1e-05) * gain))
+    products(w_res_ref, cols_sec, rows - 4)
+    for y in range(rows - 6):
+        value = first[y + 2].astype(jnp.float32) + gate(summed(y, hidden))
+        cols_third[y] = with_neighbours(value)
+    products(w_out_ref, cols_third, rows - 6)
+    for y in range(half):
+        value = summed(y, 2 * chans)
+        result[0, y] = value[:chans]
+        result[1, y] = value[chans:]
+
+    to_other = pltpu.make_async_remote_copy(
+        src_ref=result.at[peer],
+        dst_ref=arrived,
+        send_sem=send_out,
+        recv_sem=recv_out,
+        device_id=(peer, s),
+        device_id_type=MESH,
+    )
+    to_other.start()
+
+    for copy in station_copies:
+        copy.wait()
+    lanes = pack_ref.shape[1]
+    row_iota = lax.broadcasted_iota(jnp.int32, (strip, lanes), 0).astype(jnp.float32)
+    col_iota = lax.broadcasted_iota(jnp.int32, (width, lanes), 0).astype(jnp.float32)
+    top = (s * strip).astype(jnp.float32)
+    terms = chans + 1
+    for d in range(space):
+        block = sta[d]
+        at_row = jnp.where(row_iota == block[terms : terms + 1] - top, 1.0, 0.0)
+        at_col = jnp.where(col_iota == block[terms + 1 : terms + 2], 1.0, 0.0)
+        right_hand[:, d * lanes : (d + 1) * lanes] = at_col.astype(jnp.bfloat16)
+        for k in range(terms):
+            spread = block[k : k + 1] * at_row
+            coarse = spread.astype(jnp.bfloat16)
+            fine = (spread - coarse.astype(jnp.float32)).astype(jnp.bfloat16)
+            left_hand[k * strip : (k + 1) * strip, d * lanes : (d + 1) * lanes] = coarse
+            left_hand[
+                (terms + k) * strip : (terms + k + 1) * strip, d * lanes : (d + 1) * lanes
+            ] = fine
+    placed = lax.dot_general(
+        left_hand[...],
+        right_hand[...],
+        (((1,), (1,)), ((), ())),
+        preferred_element_type=jnp.float32,
+    )
+    pull_ref[...] = placed[: terms * strip] + placed[terms * strip :]
+
+    den_ref[pl.ds(half * t, half)] = result[t]
+    to_peer.wait_send()
+    to_after.wait_send()
+    to_before.wait_send()
+    to_other.wait()
+    den_ref[pl.ds(half * peer, half)] = arrived[...]
+
+
+def local_fused(
+    noisy_state,
+    fresh_noise,
+    level_index,
+    station_obs,
+    obs_variance,
+    station_owner,
+    station_cell,
+    conv_in,
+    conv_mid,
+    conv_res,
+    conv_out,
+    in_bias,
+    noise_embed,
+    norm_gain,
+):
+    steps, layers, strip, width = noisy_state.shape
+    chans = steps * layers
+    hidden = in_bias.shape[0]
+    space = lax.axis_size("space")
+    count = station_cell.shape[0]
+    noise_scale = scale_at(level_index[0])
+    next_scale = scale_at(level_index[0] - 1)
+    bias = in_bias + noise_embed * jnp.log(10.0 * noise_scale)
+    scaled = (noisy_state / jnp.sqrt(1.0 + noise_scale * noise_scale)).astype(jnp.bfloat16)
+    scaled = scaled.reshape(chans, strip, width).transpose(1, 0, 2)
+    weight = 1.0 / (obs_variance + noise_scale * noise_scale)
+    where_row = station_owner[:, 0] * strip + station_cell // width
+    where_col = station_cell % width
+    terms = chans + 1
+    packed_rows = -(-(terms + 2) // 8) * 8
+    pack = jnp.concatenate(
+        [
+            station_obs.reshape(chans, count) * weight[None],
+            weight[None],
+            where_row.astype(jnp.float32)[None],
+            where_col.astype(jnp.float32)[None],
+            jnp.zeros((packed_rows - terms - 2, count), jnp.float32),
+        ],
+        axis=0,
+    )
+    half = strip // 2
+    rows = half + 2 * HALO
+    vmem = pl.BlockSpec(memory_space=pltpu.VMEM)
+    den, pull = pl.pallas_call(
+        lambda *refs: fused_kernel(space, *refs),
+        out_shape=(
+            jax.ShapeDtypeStruct((strip, chans, width), jnp.float32),
+            jax.ShapeDtypeStruct((terms * strip, width), jnp.float32),
+        ),
+        in_specs=[vmem] * 8,
+        out_specs=(vmem, vmem),
+        scratch_shapes=[
+            pltpu.VMEM((2, rows, chans, width), jnp.bfloat16),
+            pltpu.VMEM((space, packed_rows, count), jnp.float32),
+            pltpu.VMEM((rows, 6 * chans, width), jnp.bfloat16),
+            pltpu.VMEM((rows - 2, 3 * hidden, width), jnp.bfloat16),
+            pltpu.VMEM((rows - 4, 3 * hidden, width), jnp.bfloat16),
+            pltpu.VMEM((rows - 6, 3 * hidden, width), jnp.bfloat16),
+            pltpu.VMEM((rows, 3 * hidden, width), jnp.float32),
+            pltpu.VMEM((rows - 2, hidden, width), jnp.bfloat16),
+            pltpu.VMEM((2, half, chans, width), jnp.float32),
+            pltpu.VMEM((half, chans, width), jnp.float32),
+            pltpu.VMEM((2 * terms * strip, space * count), jnp.bfloat16),
+            pltpu.VMEM((width, space * count), jnp.bfloat16),
+            pltpu.SemaphoreType.DMA((3,)),
+            pltpu.SemaphoreType.DMA((3,)),
+            pltpu.SemaphoreType.DMA((space,)),
+            pltpu.SemaphoreType.DMA((space,)),
+            pltpu.SemaphoreType.DMA,
+            pltpu.SemaphoreType.DMA,
+        ],
+        compiler_params=pltpu.CompilerParams(
+            collective_id=0, has_side_effects=True, vmem_limit_bytes=40 * 1024 * 1024
+        ),
+        name="score_and_stations",
+    )(
+        scaled,
+        pack,
+        conv_in.reshape(-1, conv_in.shape[2]),
+        conv_mid.reshape(-1, conv_mid.shape[2]),
+        conv_res.reshape(-1, conv_res.shape[2]),
+        conv_out.reshape(-1, conv_out.shape[2]),
+        bias[:, None],
+        norm_gain[:, None],
+    )
+    window_out = den.transpose(1, 0, 2).reshape(noisy_state.shape)
+    estimate = noisy_state - noise_scale * window_out
+    pull = pull.reshape(terms, strip, width)
+    observed = pull[:chans].reshape(noisy_state.shape)
+    total = observed - estimate * pull[chans]
+    return estimate + noise_scale * noise_scale * total + next_scale * fresh_noise
+
+
 def solution(mesh):
     placed = (
         P("tm", None, "space", None),
@@ -172,6 +473,7 @@
         P(),
         P(),
     )
+    pair = mesh.shape["tm"] == 2
     return jax.shard_map(
-        local, mesh=mesh, in_specs=placed, out_specs=P("tm", None, "space", None), check_vma=False
-    )
+        local_fused if pair else local, mesh=mesh, in_specs=placed, out_specs=P("tm", None, "space", None), check_vma=False
+    )

time: 83.3 us -> 24.3 us (0.29)
  starting transfers between devices: 40.3 us -> 0 us
  Pallas kernels: 0 us -> 15.4 us
  other arithmetic: 15.8 us -> 4.12 us
  waiting for transfers between devices: 9.03 us -> 0 us
  local copies, waits for them, and re-layouts: 11.5 us -> 3.56 us
  matrix products: 4.83 us -> 0 us
    ppermute x10 -> x0, starting transfers between devices: 23.9 us -> none  [the longest x4 17.1 us: extended_2(): lax.ppermute(head, axis, [((i + 1) % count, i) for i in range(count)])]
    all_to_all x3 -> x0, starting transfers between devices: 16.4 us -> none  [the longest x1 7.39 us: local(): lax.all_to_all(cell_slots, 'space', split_axis=1, concat_axis=1, tiled=True)]
    pallas_call x0 -> x1, Pallas kernels: none -> 15.4 us  [local_fused(): pl.pallas_call(lambda *refs: fused_kernel(space, *refs), out_shape=(jax.S...]
    scatter-add x1 -> x0, other arithmetic: 6.21 us -> none  [local(): pull = jnp.zeros_like(flat).at[:, spot].add(misfit)]
    all_to_all x3 -> x0, waiting for transfers between devices: 6.13 us -> none  [the longest x1 6.12 us: local(): lax.all_to_all(value_slots, 'space', split_axis=1, concat_axis=1, tiled=T...]
    concatenate x9 -> x0, other arithmetic: 5.11 us -> none  [the longest x4 4.2 us: conv_rows(): jnp.concatenate([jnp.roll(padded, 1 - col_tap, axis=3) for col_tap in ran...]
    dot_general x12 -> x0, matrix products: 4.83 us -> none  [conv_rows(): jnp.einsum('oc,ncyx->noyx', weight[row_tap], stacked[:, :, row_tap:row_ta...]
    scatter x3 -> x0, local copies, waits for them, and re-layouts: 3.15 us -> none  [the longest x1 1.1 us: local(): jnp.full((1, slot_count), -1, jnp.int32).at[0, slot].set(station_cell)]
  transfers between devices with their start and end apart: 13 -> 0, of which waited for: 4 -> 0; matrix products, arithmetic and copies ran while one was open for 24% -> 0% of each run, Pallas kernels for 0% -> 0%
where the time goes in v1:
time: 24.3 us; the launch traced here: 24 us
  Pallas kernels  15.4 us (63%)
  other arithmetic  4.12 us (17%)
  local copies, waits for them, and re-layouts  3.56 us (15%)
  between operations  0.97 us (4%)
    pallas_call x1, Pallas kernels, local_fused(): pl.pallas_call(lambda *refs: fused_kernel(space, *refs), out_shape=(jax.S...  15.4 us
    unnamed x11, local copies, waits for them, and re-layouts  2.62 us
    broadcast_in_dim x1, local copies, waits for them, and re-layouts, local_fused(): norm_gain[:, None]  0.74 us
    add x1, other arithmetic, local_fused(): estimate + noise_scale * noise_scale * total + next_scale * fresh_noise  0.71 us
    mul x1, other arithmetic, local_fused(): station_obs.reshape(chans, count) * weight[None]  0.69 us
    broadcast_in_dim x1, other arithmetic, local_fused(): where_col.astype(jnp.float32)[None]  0.69 us
    broadcast_in_dim x1, other arithmetic, local_fused(): bias[:, None]  0.68 us
    div x1, other arithmetic, local_fused(): weight = 1.0 / (obs_variance + noise_scale * noise_scale)  0.66 us

profile of v1, /device:TPU:0, one launch (start us, length us, event | category | flops | bytes accessed | tf_op | source)
XLA Modules:
  0.0 24.0 jit_solution(10078547642907711653)
XLA Ops:
  0.0 0.0 copy-start.3
  0.9 0.7 %add_bitcast_fusion = f32[64,1]{0,1:T(1,128)S(1)} fusion(f32[64]{0:T(128)} %param.25, f32[64]{0:T(128)} %param.26, f32[]{:T(128)} %bitcast.13), kind=kLoop, calls=%fused_computation.15 | loop fusion | flops 128 | bytes 772 | tf_op jit(solution)/shard_map/broadcast_in_dim | solution.py:448
  1.5 0.7 %fusion.4 = f32[1,128]{1,0:T(1,128)S(1)} fusion(f32[128]{0:T(128)} %param.18, f32[]{:T(128)} %bitcast.1), kind=kLoop, calls=%fused_computation.17 | loop fusion | flops 256 | bytes 1028 | tf_op jit(solution)/shard_map/broadcast_in_dim | solution.py:398
  2.2 0.7 %add_divide_fusion = f32[128]{0:T(128)S(1)} fusion(f32[128]{0:T(128)} %param.18, f32[]{:T(128)} %bitcast.1), kind=kLoop, calls=%fused_computation.16 | loop fusion | flops 256 | bytes 1028 | tf_op jit(solution)/shard_map/div | solution.py:391
  2.9 0.7 %fusion.1 = (f32[1,128]{1,0:T(1,128)S(1)}, f32[1,128]{1,0:T(1,128)S(1)}) fusion(s32[128]{0:T(128)} %param.20, s32[128,1]{0,1:T(1,128)} %param.19), kind=kLoop, calls=%fused_computation.11 | loop fusion | flops 2944 | bytes 2048 | tf_op jit(solution)/shard_map/broadcast_in_dim | solution.py:401
  3.6 0.7 %broadcast_multiply_fusion = f32[8,128]{1,0:T(8,128)S(1)} fusion(f32[8,128]{1,0:T(8,128)} %bitcast.40, f32[128]{0:T(128)S(1)} %add_divide_fusion), kind=kLoop, calls=%fused_computation.4 | loop fusion | flops 1024 | bytes 8704 | tf_op jit(solution)/shard_map/mul | solution.py:398
  4.3 0.1 copy.17.refs_6_
  4.4 0.7 %copy.18.refs_7_ = f32[64,1]{1,0:T(8,128)S(1)} copy(f32[64,1]{0,1:T(1,128)} %bitcast.41) | data formatting | bytes 512 | tf_op jit(solution)/shard_map/broadcast_in_dim | solution.py:449
  5.1 0.9 %copy.16 = bf16[3,64,48]{2,1,0:T(8,128)(2,1)S(1)} copy(bf16[3,64,48]{1,2,0:T(8,128)(2,1)} %param.21) | data formatting | bytes 36864 | tf_op args[7]
  6.0 0.0 copy-done.3
  6.0 0.0 copy-start.1
  6.0 0.0 copy-start
  6.0 0.0 copy-start.2
  6.1 0.8 %copy-done.1 = bf16[3,64,192]{2,1,0:T(8,128)(2,1)S(1)} copy-done((bf16[3,64,192]{2,1,0:T(8,128)(2,1)S(1)}, bf16[3,64,192]{2,1,0:T(8,128)(2,1)}, u32[]{:S(2)}) %copy-start.1) | copy-done | bytes 73752
  6.9 0.1 copy-done
  6.9 0.0 copy-done.2
  6.9 15.4 %score_and_stations.1 = (f32[16,8,256]{2,1,0:T(8,128)S(1)}, f32[144,256]{1,0:T(8,128)S(1)}) custom-call(bf16[16,8,256]{2,1,0:T(8,128)(2,1)S(1)} %bitcast.32, f32[16,128]{1,0:T(8,128)S(1)} %concatenate.3.refs_1_, bf16[192,48]{1,0:T(8,128)(2,1)S(1)} %bitcast.33, bf16[192,192]{1,0:T(8,128)(2,1)S(1)} %bitcast.34, bf16[192,192]{1,0:T(8,128)(2,1)S(1)} %bitcast.35, ...), custom_call_target="tpu_custom_call" | custom-call | tf_op jit(solution)/shard_map/score_and_stations/pallas_call | solution.py:409
  22.4 0.0 copy-start.4
  22.4 0.9 %copy-done.4 = f32[4,2,16,256]{3,2,1,0:T(8,128)S(1)} copy-done((f32[4,2,16,256]{3,2,1,0:T(8,128)S(1)}, f32[4,2,16,256]{3,2,1,0:T(8,128)}, u32[]{:S(2)}) %copy-start.4) | copy-done | bytes 131096
  23.3 0.7 %multiply_add_fusion = f32[4,2,16,256]{3,2,1,0:T(8,128)} fusion(f32[4,2,16,256]{3,2,1,0:T(8,128)S(1)} %copy-done.4, f32[4,2,16,256]{3,2,1,0:T(8,128)S(1)} %bitcast.38, f32[4,2,16,256]{3,2,1,0:T(8,128)S(1)} %copy-done.3, f32[4,2,16,256]{3,2,1,0:T(8,128)S(1)} %bitcast.37, f32[]{:T(128)} %bitcast.19, f32[16,256]{1,0:T(8,128)S(1)} %slice.9, f32[]{:T(128)} %bitcast.1), kind=kLoop, calls=%fused_computation | loop fusion | flops 229376 | bytes 671752 | tf_op jit(solution)/shard_map/add | solution.py:456
  (8 shorter events, 0.1 us)
Async XLA Ops:
  0.0 6.0 %copy-start.3 = (f32[4,2,16,256]{3,2,1,0:T(8,128)S(1)}, f32[4,2,16,256]{3,2,1,0:T(8,128)}, u32[]{:S(2)}) copy-start(f32[4,2,16,256]{3,2,1,0:T(8,128)} %param.14) | copy-start | bytes 393220
  6.0 0.9 %copy-start.1 = (bf16[3,64,192]{2,1,0:T(8,128)(2,1)S(1)}, bf16[3,64,192]{2,1,0:T(8,128)(2,1)}, u32[]{:S(2)}) copy-start(bf16[3,64,192]{2,1,0:T(8,128)(2,1)} %param.23) | copy-start | bytes 221188
  6.0 0.9 %copy-start = (bf16[3,64,192]{2,1,0:T(8,128)(2,1)S(1)}, bf16[3,64,192]{2,1,0:T(8,128)(2,1)}, u32[]{:S(2)}) copy-start(bf16[3,64,192]{2,1,0:T(8,128)(2,1)} %param.22) | copy-start | bytes 221188
  6.0 0.9 %copy-start.2 = (bf16[3,16,192]{2,1,0:T(8,128)(2,1)S(1)}, bf16[3,16,192]{2,1,0:T(8,128)(2,1)}, u32[]{:S(2)}) copy-start(bf16[3,16,192]{2,1,0:T(8,128)(2,1)} %param.24) | copy-start | bytes 55300
  22.4 0.9 %copy-start.4 = (f32[4,2,16,256]{3,2,1,0:T(8,128)S(1)}, f32[4,2,16,256]{3,2,1,0:T(8,128)}, u32[]{:S(2)}) copy-start(f32[4,2,16,256]{3,2,1,0:T(8,128)} %param.15) | copy-start | bytes 393220

commit v2 on v1

--- a/solution.py
+++ b/solution.py
@@ -174,16 +174,30 @@
 
 def fused_kernel(
     space,
-    scaled_ref,
-    pack_ref,
+    level_ref,
+    noisy_hbm,
+    fresh_hbm,
+    obs_ref,
+    variance_ref,
+    owner_ref,
+    cell_ref,
     w_in_ref,
+    w_mid_hbm,
+    w_res_hbm,
+    w_out_hbm,
+    bias_ref,
+    embed_ref,
+    gain_ref,
+    next_ref,
+    noisy_ref,
+    fresh_ref,
+    w_in_rows,
     w_mid_ref,
     w_res_ref,
     w_out_ref,
-    bias_ref,
-    gain_ref,
-    den_ref,
-    pull_ref,
+    load_sem,
+    scaled_ref,
+    pack_ref,
     win,
     sta,
     cols_in,
@@ -194,6 +208,8 @@
     first,
     result,
     arrived,
+    whole,
+    pulls,
     left_hand,
     right_hand,
     send_halo,
@@ -209,13 +225,26 @@
     after = lax.rem(s + 1, space)
     before = lax.rem(s + space - 1, space)
     diagonal = lax.rem(s + space - 1 + 2 * t, space)
-    strip = scaled_ref.shape[0]
+    chans, strip, width = noisy_ref.shape
     half = strip // 2
     span = half + HALO
-    chans = scaled_ref.shape[1]
-    hidden = bias_ref.shape[0]
-    width = scaled_ref.shape[2]
-
+    hidden = bias_ref.shape[1]
+    count = cell_ref.shape[1]
+
+    loads = [
+        pltpu.make_async_copy(source, target, load_sem.at[k])
+        for k, (source, target) in enumerate(
+            (
+                (noisy_hbm, noisy_ref),
+                (w_mid_hbm, w_mid_ref),
+                (w_res_hbm, w_res_ref),
+                (w_out_hbm, w_out_ref),
+                (fresh_hbm, fresh_ref),
+            )
+        )
+    ]
+    for load in loads:
+        load.start()
     barrier = pltpu.get_barrier_semaphore()
     pl.semaphore_signal(barrier, inc=1, device_id=(peer, s), device_id_type=MESH)
     pl.semaphore_signal(barrier, inc=1, device_id=(peer, diagonal), device_id_type=MESH)
@@ -223,6 +252,28 @@
         pl.semaphore_signal(
             barrier, inc=1, device_id=(t, lax.rem(s + d, space)), device_id_type=MESH
         )
+
+    noise = scale_at(jnp.full((1, width), level_ref[0], jnp.int32))
+    following = scale_at(jnp.full((1, width), level_ref[0] - 1, jnp.int32))
+    spread_out = jnp.sqrt(1.0 + noise * noise)
+    loads[0].wait()
+    for y in range(strip):
+        scaled_ref[y] = (noisy_ref[:, y, :] / spread_out).astype(jnp.bfloat16)
+    noise_sta = noise[:, :1]
+    weight = 1.0 / (variance_ref[...] + noise_sta * noise_sta)
+    cell = cell_ref[...].astype(jnp.float32)
+    cell_row = jnp.floor((cell + 0.5) / width)
+    sort = lax.broadcasted_iota(jnp.int32, (8, count), 0)
+    pack_ref[0:chans] = obs_ref[...] * weight
+    pack_ref[chans : chans + 8] = jnp.where(
+        sort == 0,
+        weight,
+        jnp.where(
+            sort == 1,
+            owner_ref[...].astype(jnp.float32) * strip + cell_row,
+            jnp.where(sort == 2, cell - cell_row * width, 0.0),
+        ),
+    )
     pl.semaphore_wait(barrier, space + 1)
 
     to_peer = pltpu.make_async_remote_copy(
@@ -267,6 +318,13 @@
     sta[0] = pack_ref[...]
     win[t, pl.ds(HALO * (1 - t), span)] = scaled_ref[pl.ds(HALO * t, span)]
 
+    for tap in range(3):
+        w_in_rows[hidden * tap : hidden * (tap + 1)] = (
+            w_in_ref[tap].astype(jnp.float32).T.astype(jnp.bfloat16)
+        )
+    for load in loads[1:4]:
+        load.wait()
+
     def landed(dst, sem):
         pltpu.make_async_copy(dst, dst, sem).wait()
 
@@ -276,8 +334,9 @@
     landed(win.at[1, pl.ds(edge, HALO)], recv_halo.at[2])
 
     rows = half + 2 * HALO
-    bias = jnp.broadcast_to(bias_ref[...], (hidden, width))
-    gain = jnp.broadcast_to(gain_ref[...], (hidden, width))
+    shift = jnp.log(10.0 * noise)[:, :hidden]
+    bias = jnp.broadcast_to(bias_ref[...] + embed_ref[...] * shift, (width, hidden)).T
+    gain = jnp.broadcast_to(gain_ref[...], (width, hidden)).T
 
     def products(weight_ref, columns, count):
         outs = weight_ref.shape[0]
@@ -296,7 +355,7 @@
             [win[0, r].astype(jnp.float32), win[1, r].astype(jnp.float32)], axis=0
         )
         cols_in[r] = with_neighbours(both)
-    products(w_in_ref, cols_in, rows)
+    products(w_in_rows, cols_in, rows)
     for y in range(rows - 2):
         value = gate(summed(y, hidden) + bias)
         first[y] = value.astype(jnp.bfloat16)
@@ -338,28 +397,43 @@
         at_row = jnp.where(row_iota == block[terms : terms + 1] - top, 1.0, 0.0)
         at_col = jnp.where(col_iota == block[terms + 1 : terms + 2], 1.0, 0.0)
         right_hand[:, d * lanes : (d + 1) * lanes] = at_col.astype(jnp.bfloat16)
-        for k in range(terms):
-            spread = block[k : k + 1] * at_row
+        span_of = slice(d * lanes, (d + 1) * lanes)
+
+        def put(at, spread):
             coarse = spread.astype(jnp.bfloat16)
             fine = (spread - coarse.astype(jnp.float32)).astype(jnp.bfloat16)
-            left_hand[k * strip : (k + 1) * strip, d * lanes : (d + 1) * lanes] = coarse
-            left_hand[
-                (terms + k) * strip : (terms + k + 1) * strip, d * lanes : (d + 1) * lanes
-            ] = fine
+            left_hand[at : at + spread.shape[0], span_of] = coarse
+            at = terms * strip + at
+            left_hand[at : at + spread.shape[0], span_of] = fine
+
+        for y in range(0, strip, 2):
+            put(
+                chans * y,
+                jnp.concatenate(
+                    [block[:chans] * at_row[y : y + 1], block[:chans] * at_row[y + 1 : y + 2]],
+                    axis=0,
+                ),
+            )
+        put(chans * strip, block[chans : chans + 1] * at_row)
     placed = lax.dot_general(
         left_hand[...],
         right_hand[...],
         (((1,), (1,)), ((), ())),
         preferred_element_type=jnp.float32,
     )
-    pull_ref[...] = placed[: terms * strip] + placed[terms * strip :]
-
-    den_ref[pl.ds(half * t, half)] = result[t]
+    pulls[...] = placed[: terms * strip] + placed[terms * strip :]
     to_peer.wait_send()
     to_after.wait_send()
     to_before.wait_send()
     to_other.wait()
-    den_ref[pl.ds(half * peer, half)] = arrived[...]
+    whole[pl.ds(half * t, half)] = result[t]
+    whole[pl.ds(half * peer, half)] = arrived[...]
+    loads[4].wait()
+    for y in range(strip):
+        estimate = noisy_ref[:, y, :] - noise * whole[y]
+        base = chans * strip + y
+        pull = pulls[chans * y : chans * (y + 1)] - estimate * pulls[base : base + 1]
+        next_ref[y] = estimate + noise * noise * pull + following * fresh_ref[:, y, :]
 
 
 def local_fused(
@@ -383,38 +457,30 @@
     hidden = in_bias.shape[0]
     space = lax.axis_size("space")
     count = station_cell.shape[0]
-    noise_scale = scale_at(level_index[0])
-    next_scale = scale_at(level_index[0] - 1)
-    bias = in_bias + noise_embed * jnp.log(10.0 * noise_scale)
-    scaled = (noisy_state / jnp.sqrt(1.0 + noise_scale * noise_scale)).astype(jnp.bfloat16)
-    scaled = scaled.reshape(chans, strip, width).transpose(1, 0, 2)
-    weight = 1.0 / (obs_variance + noise_scale * noise_scale)
-    where_row = station_owner[:, 0] * strip + station_cell // width
-    where_col = station_cell % width
     terms = chans + 1
-    packed_rows = -(-(terms + 2) // 8) * 8
-    pack = jnp.concatenate(
-        [
-            station_obs.reshape(chans, count) * weight[None],
-            weight[None],
-            where_row.astype(jnp.float32)[None],
-            where_col.astype(jnp.float32)[None],
-            jnp.zeros((packed_rows - terms - 2, count), jnp.float32),
-        ],
-        axis=0,
-    )
+    packed_rows = chans + 8
     half = strip // 2
     rows = half + 2 * HALO
+    hbm = pl.BlockSpec(memory_space=pltpu.MemorySpace.HBM)
     vmem = pl.BlockSpec(memory_space=pltpu.VMEM)
-    den, pull = pl.pallas_call(
+    result = pl.pallas_call(
         lambda *refs: fused_kernel(space, *refs),
-        out_shape=(
-            jax.ShapeDtypeStruct((strip, chans, width), jnp.float32),
-            jax.ShapeDtypeStruct((terms * strip, width), jnp.float32),
-        ),
-        in_specs=[vmem] * 8,
-        out_specs=(vmem, vmem),
+        out_shape=jax.ShapeDtypeStruct((strip, chans, width), jnp.float32),
+        in_specs=[pl.BlockSpec(memory_space=pltpu.SMEM), hbm, hbm]
+        + [vmem] * 5
+        + [hbm] * 3
+        + [vmem] * 3,
+        out_specs=vmem,
         scratch_shapes=[
+            pltpu.VMEM((chans, strip, width), jnp.float32),
+            pltpu.VMEM((chans, strip, width), jnp.float32),
+            pltpu.VMEM((3 * hidden, conv_in.shape[2]), jnp.bfloat16),
+            pltpu.VMEM((3 * hidden, 3 * hidden), jnp.bfloat16),
+            pltpu.VMEM((3 * hidden, 3 * hidden), jnp.bfloat16),
+            pltpu.VMEM((6 * chans, 3 * hidden), jnp.bfloat16),
+            pltpu.SemaphoreType.DMA((5,)),
+            pltpu.VMEM((strip, chans, width), jnp.bfloat16),
+            pltpu.VMEM((packed_rows, count), jnp.float32),
             pltpu.VMEM((2, rows, chans, width), jnp.bfloat16),
             pltpu.VMEM((space, packed_rows, count), jnp.float32),
             pltpu.VMEM((rows, 6 * chans, width), jnp.bfloat16),
@@ -425,6 +491,8 @@
             pltpu.VMEM((rows - 2, hidden, width), jnp.bfloat16),
             pltpu.VMEM((2, half, chans, width), jnp.float32),
             pltpu.VMEM((half, chans, width), jnp.float32),
+            pltpu.VMEM((strip, chans, width), jnp.float32),
+            pltpu.VMEM((terms * strip, width), jnp.float32),
             pltpu.VMEM((2 * terms * strip, space * count), jnp.bfloat16),
             pltpu.VMEM((width, space * count), jnp.bfloat16),
             pltpu.SemaphoreType.DMA((3,)),
@@ -435,25 +503,26 @@
             pltpu.SemaphoreType.DMA,
         ],
         compiler_params=pltpu.CompilerParams(
-            collective_id=0, has_side_effects=True, vmem_limit_bytes=40 * 1024 * 1024
+            collective_id=0, has_side_effects=True
         ),
         name="score_and_stations",
     )(
-        scaled,
-        pack,
-        conv_in.reshape(-1, conv_in.shape[2]),
+        level_index,
+        noisy_state.reshape(chans, strip, width),
+        fresh_noise.reshape(chans, strip, width),
+        station_obs.reshape(chans, count),
+        obs_variance[None],
+        station_owner.reshape(1, count),
+        station_cell[None],
+        conv_in.transpose(0, 2, 1),
         conv_mid.reshape(-1, conv_mid.shape[2]),
         conv_res.reshape(-1, conv_res.shape[2]),
         conv_out.reshape(-1, conv_out.shape[2]),
-        bias[:, None],
-        norm_gain[:, None],
-    )
-    window_out = den.transpose(1, 0, 2).reshape(noisy_state.shape)
-    estimate = noisy_state - noise_scale * window_out
-    pull = pull.reshape(terms, strip, width)
-    observed = pull[:chans].reshape(noisy_state.shape)
-    total = observed - estimate * pull[chans]
-    return estimate + noise_scale * noise_scale * total + next_scale * fresh_noise
+        in_bias[None],
+        noise_embed[None],
+        norm_gain[None],
+    )
+    return result.transpose(1, 0, 2).reshape(noisy_state.shape)
 
 
 def solution(mesh):

time: 24.3 us -> 19.6 us (0.81)
  other arithmetic: 4.12 us -> 0 us
  local copies, waits for them, and re-layouts: 3.56 us -> 1.6 us
  Pallas kernels: 15.4 us -> 17.1 us
  between operations: 0.97 us -> 0.66 us
    unnamed x11 -> x0, local copies, waits for them, and re-layouts: 2.62 us -> none
    broadcast_in_dim x3 -> x0, other arithmetic: 2.02 us -> none  [the longest x1 0.69 us: local_fused(): where_col.astype(jnp.float32)[None]]
    pallas_call x1, Pallas kernels: 15.4 us -> 17.1 us  [local_fused(): pl.pallas_call(lambda *refs: fused_kernel(space, *refs), out_shape=jax.Sh...]
    reshape x1, local copies, waits for them, and re-layouts: 0.02 us -> 1.6 us  [local_fused(): return result.transpose(1, 0, 2).reshape(noisy_state.shape)]
    broadcast_in_dim x3 -> x0, local copies, waits for them, and re-layouts: 0.84 us -> none  [the longest x1 0.74 us: local_fused(): norm_gain[:, None]]
    add x1 -> x0, other arithmetic: 0.71 us -> none  [local_fused(): estimate + noise_scale * noise_scale * total + next_scale * fresh_noise]
    mul x2 -> x0, other arithmetic: 0.71 us -> none  [the longest x1 0.69 us: local_fused(): station_obs.reshape(chans, count) * weight[None]]
    div x1 -> x0, other arithmetic: 0.66 us -> none  [local_fused(): weight = 1.0 / (obs_variance + noise_scale * noise_scale)]
where the time goes in v2:
time: 19.6 us; the launch traced here: 19.4 us
  Pallas kernels  17.1 us (87%)
  local copies, waits for them, and re-layouts  1.6 us (8%)
  between operations  0.66 us (3%)
    pallas_call x1, Pallas kernels, local_fused(): pl.pallas_call(lambda *refs: fused_kernel(space, *refs), out_shape=jax.Sh...  17.1 us
    reshape x1, local copies, waits for them, and re-layouts, local_fused(): return result.transpose(1, 0, 2).reshape(noisy_state.shape)  1.6 us

profile of v2, /device:TPU:0, one launch (start us, length us, event | category | flops | bytes accessed | tf_op | source)
XLA Modules:
  0.0 19.4 jit_solution(6731317786042457297)
XLA Ops:
  0.7 17.1 %score_and_stations.1 = f32[16,8,256]{2,1,0:T(8,128)} custom-call(s32[1]{0:T(128)S(6)} %copy.17.refs_0_, f32[8,16,256]{2,1,0:T(8,128)} %bitcast.16, f32[8,16,256]{2,1,0:T(8,128)} %bitcast.17, f32[8,128]{1,0:T(8,128)} %bitcast.22, f32[1,128]{1,0:T(1,128)} %bitcast.23, s32[1,128]{1,0:T(1,128)} %bitcast.24, s32[1,128]{1,0:T(1,128)} %bitcast.25, ...), custom_call_target="tpu_custom_call" | custom-call | tf_op jit(solution)/shard_map/score_and_stations/pallas_call | solution.py:466
  17.8 1.6 %copy.16 = f32[8,16,256]{2,1,0:T(8,128)} copy(f32[8,16,256]{2,0,1:T(8,128)} %bitcast.15) | data formatting | bytes 262144 | tf_op jit(solution)/shard_map/reshape | solution.py:525
